TPU v7x, 256 devices: a whole 4x4x8 slice. The times are simulated.
256 devices in a mesh: dom: 16 (over z, x_lo), ref: 16 (over x_hi, y, core).
Axes of the slice: x: 4 (x_hi: 2, x_lo: 2; x = x_hi * 2 + x_lo), y: 4, z: 8, core: 2. Of those that a mesh axis runs over, the one named last changes fastest.
Arguments:
- particles: float32 [8192, 128], P('dom'), may hold values from -1.2 to 1.2
- references: float32 [16384, 128], P('ref'), may hold values from -1 to 1.2
Outputs:
- moved: float32 [8192, 128], P(('dom', 'ref'))
- drift: float32 [8192, 128], P(('dom', 'ref'))
All inputs are finite; a program needn't handle non-finite values.
Results may differ from a plain program's by a relative error of at most 0.00035.
Values sent between devices are 32-bit elements; how exact they have to be, the bound alone decides.
A program may use at most 64 MiB of HBM per device.

v0:
```python
import jax
import jax.numpy as jnp
from jax import lax
from jax.sharding import PartitionSpec as P

STEPS = 2
step_size = 0.5


def kernel_terms(block, others):
    inner = jnp.dot(
        block, others.T, precision=lax.Precision.HIGHEST, preferred_element_type=jnp.float32
    )
    squared = (
        jnp.sum(block * block, axis=1)[:, None]
        + jnp.sum(others * others, axis=1)[None, :]
        - 2.0 * inner
    )
    weights = jnp.exp(-0.5 * squared)
    pulled = jnp.dot(
        weights, others, precision=lax.Precision.HIGHEST, preferred_element_type=jnp.float32
    )
    return (pulled, jnp.sum(weights, axis=1))


def partial_gradient(block, own_rows, references, count_p, count_r):
    pulled, summed = kernel_terms(block, lax.all_gather(own_rows, "dom", axis=0, tiled=True))
    pull_r, sum_r = kernel_terms(block, references)
    return (pulled - summed[:, None] * block) / count_p - (
        pull_r - sum_r[:, None] * block
    ) / count_r


def on_device(particles, references):
    n_ref = lax.axis_size("ref")
    n_dom = lax.axis_size("dom")
    rows = particles.shape[0] // n_ref
    count_p = particles.shape[0] * n_dom
    count_r = references.shape[0] * n_ref
    offset = lax.axis_index("ref") * rows
    start_rows = lax.dynamic_slice_in_dim(particles, offset, rows, 0)
    block = particles
    own_rows = start_rows
    for step in range(STEPS):
        partial_value = partial_gradient(block, own_rows, references, count_p, count_r)
        gradient = lax.psum(partial_value, "ref")
        block = block - step_size * gradient
        own_rows = lax.dynamic_slice_in_dim(block, offset, rows, 0)
    return (own_rows, (own_rows - start_rows) / step_size)


def solution(mesh):
    placed = (P("dom", None), P("ref", None))
    return jax.shard_map(
        on_device,
        mesh=mesh,
        in_specs=placed,
        out_specs=(P(("dom", "ref"), None), P(("dom", "ref"), None)),
        check_vma=False,
    )
```

profile of v0, /device:TPU:1, one launch (start us, length us, event | category | flops | bytes accessed | tf_op | source)
XLA Modules:
  0.0 391.9 jit_solution(12961687768505106673)
XLA Ops:
  7.2 0.0 copy-start
  7.2 0.0 copy-start.1
  7.2 0.0 all-reduce.3.cloned.1.call-start
  7.2 1.2 multiply_reduce_fusion.4
  8.4 1.2 multiply_reduce_fusion
  9.7 0.7 constant_dynamic-slice_fusion.1
  10.4 31.7 %all_gather.6 = f32[512,128]{1,0:T(8,128)S(1)} all-gather(f32[32,128]{1,0:T(8,128)S(1)} %constant_dynamic-slice_fusion.1), channel_id=1, replica_groups=mesh['dom'=16,'ref'=16] {'dom'}, dimensions={0}, use_global_device_ids=true | all-gather | bytes 278528 | tf_op jit(solution)/shard_map/all_gather | solution.py:27
  42.1 0.1 multiply_reduce_fusion.3
  42.2 2.1 fusion.15
  44.3 0.0 copy-done
  44.4 0.0 copy-done.1
  44.4 2.3 fusion.16
  46.7 1.8 fusion.12
  48.5 2.5 fusion.9
  51.0 0.0 all-reduce.3.cloned.1.call-update
  51.1 0.0 all-reduce.5.cloned.1.call-start
  51.1 148.4 %all-reduce.3.cloned.1.call-done = f32[512,128]{1,0:T(8,128)} async-done(((f32[512,128]{1,0:T(8,128)}), f32[512,128]{1,0:T(8,128)}) %all-reduce.3.cloned.1.call-update) | async-done | bytes 262160 | tf_op jit(solution)/shard_map/psum | solution.py:46
  199.5 1.1 multiply_reduce_fusion.2
  200.7 27.7 %all_gather.7 = f32[512,128]{1,0:T(8,128)S(1)} all-gather(f32[32,128]{1,0:T(8,128)S(1)} %constant_dynamic-slice_fusion), channel_id=1, replica_groups=mesh['dom'=16,'ref'=16] {'dom'}, dimensions={0}, use_global_device_ids=true | all-gather | bytes 278528 | tf_op jit(solution)/shard_map/all_gather | solution.py:27
  228.4 0.1 multiply_reduce_fusion.1
  228.5 2.3 fusion.18
  230.8 1.2 fusion.17
  232.1 1.8 fusion.11
  233.9 2.5 fusion.10
  236.4 0.0 all-reduce.5.cloned.1.call-update
  236.5 147.3 %all-reduce.5.cloned.1.call-done = f32[512,128]{1,0:T(8,128)} async-done(((f32[512,128]{1,0:T(8,128)}), f32[512,128]{1,0:T(8,128)}) %all-reduce.5.cloned.1.call-update) | async-done | bytes 262160 | tf_op jit(solution)/shard_map/psum | solution.py:46
  383.7 1.3 subtract_multiply_fusion
  (1 shorter events, 0.0 us)
Async XLA Ops:
  7.2 37.2 %copy-start = (f32[512,128]{1,0:T(8,128)S(1)}, f32[512,128]{1,0:T(8,128)}, u32[]{:S(2)}) copy-start(f32[512,128]{1,0:T(8,128)} %param.2) | copy-start | bytes 786436
  7.2 37.2 %copy-start.1 = (f32[1024,128]{1,0:T(8,128)S(1)}, f32[1024,128]{1,0:T(8,128)}, u32[]{:S(2)}) copy-start(f32[1024,128]{1,0:T(8,128)} %param.3) | copy-start | bytes 1572868
  7.2 192.4 %all-reduce.3.cloned.1.call-start = ((), (), s32[]{:S(2)}) async-start(), calls=%async_computation | async-start | bytes 524288 | tf_op jit(solution)/shard_map/psum | solution.py:46
  51.1 332.7 %all-reduce.5.cloned.1.call-start = ((), (), s32[]{:S(2)}) async-start(), calls=%async_computation.1 | async-start | bytes 524288 | tf_op jit(solution)/shard_map/psum | solution.py:46
Sparse Core Ops, SparseCore 0:
  51.2 148.3 all-reduce.2
  236.6 147.0 all-reduce.4
where the time goes:
time: 392 us
  waiting for transfers between devices  296 us (76%)
  blocking collectives  59.4 us (15%)
  matrix products  16.7 us (4%)
  between operations  14.1 us (4%)
  other arithmetic  5.12 us (1%)
    psum x2, waiting for transfers between devices, on_device(): gradient = lax.psum(partial_value, 'ref')  296 us
    all_gather x2, blocking collectives, partial_gradient(): lax.all_gather(own_rows, 'dom', axis=0, tiled=True)  59.4 us
    dot_general x4, matrix products, kernel_terms(): jnp.dot(weights, others, precision=lax.Precision.HIGHEST, preferred_eleme...  8.73 us
    dot_general x4, matrix products, kernel_terms(): jnp.dot(block, others.T, precision=lax.Precision.HIGHEST, preferred_eleme...  7.95 us
  transfers between devices with their start and end apart: 2, of which 2 were waited for; matrix products, arithmetic and copies ran while one was open for 0% of the time, Pallas kernels for 0%

commit v1 on v0

--- a/solution.py
+++ b/solution.py
@@ -43,7 +43,7 @@
     own_rows = start_rows
     for step in range(STEPS):
         partial_value = partial_gradient(block, own_rows, references, count_p, count_r)
-        gradient = lax.psum(partial_value, "ref")
+        gradient = jnp.sum(lax.all_gather(partial_value, "ref"), axis=0)
         block = block - step_size * gradient
         own_rows = lax.dynamic_slice_in_dim(block, offset, rows, 0)
     return (own_rows, (own_rows - start_rows) / step_size)

time: 392 us -> 227 us (0.58)
  waiting for transfers between devices: 296 us -> 128 us
    psum x2 -> x0, waiting for transfers between devices: 296 us -> none  [on_device(): gradient = lax.psum(partial_value, 'ref')]
    all_gather x0 -> x2, waiting for transfers between devices: none -> 128 us  [on_device(): gradient = jnp.sum(lax.all_gather(partial_value, 'ref'), axis=0)]
    reduce_sum x0 -> x2, other arithmetic: none -> 4.81 us  [on_device(): gradient = jnp.sum(lax.all_gather(partial_value, 'ref'), axis=0)]
where the time goes in v1:
time: 227 us; the launch traced here: 226 us
  waiting for transfers between devices  128 us (56%)
  blocking collectives  58.9 us (26%)
  matrix products  16.5 us (7%)
  between operations  14.1 us (6%)
  other arithmetic  8.28 us (4%)
    all_gather x2, waiting for transfers between devices, on_device(): gradient = jnp.sum(lax.all_gather(partial_value, 'ref'), axis=0)  128 us
    all_gather x2, blocking collectives, partial_gradient(): lax.all_gather(own_rows, 'dom', axis=0, tiled=True)  58.9 us
    dot_general x4, matrix products, kernel_terms(): jnp.dot(weights, others, precision=lax.Precision.HIGHEST, preferred_eleme...  8.59 us
    dot_general x4, matrix products, kernel_terms(): jnp.dot(block, others.T, precision=lax.Precision.HIGHEST, preferred_eleme...  7.88 us
    reduce_sum x2, other arithmetic, on_device(): gradient = jnp.sum(lax.all_gather(partial_value, 'ref'), axis=0)  4.81 us
  transfers between devices with their start and end apart: 2, of which 2 were waited for; matrix products, arithmetic and copies ran while one was open for 0% of the time, Pallas kernels for 0%

profile of v1, /device:TPU:1, one launch (start us, length us, event | category | flops | bytes accessed | tf_op | source)
XLA Modules:
  0.0 226.5 jit_solution(16002464640386293017)
XLA Ops:
  7.2 0.0 copy-start
  7.2 0.0 copy-start.1
  7.2 0.0 all-gather.5.cloned.1.call-start
  7.2 1.2 multiply_reduce_fusion.4
  8.4 1.2 multiply_reduce_fusion
  9.7 0.7 constant_dynamic-slice_fusion.1
  10.4 31.7 %all_gather.18 = f32[512,128]{1,0:T(8,128)S(1)} all-gather(f32[32,128]{1,0:T(8,128)S(1)} %constant_dynamic-slice_fusion.1), channel_id=1, replica_groups=mesh['dom'=16,'ref'=16] {'dom'}, dimensions={0}, use_global_device_ids=true | all-gather | bytes 278528 | tf_op jit(solution)/shard_map/all_gather | solution.py:27
  42.1 0.1 multiply_reduce_fusion.3
  42.2 2.1 fusion.15
  44.3 0.0 copy-done
  44.4 0.0 copy-done.1
  44.4 2.3 %fusion.16 = (f32[512]{0:T(512)S(1)}, f32[512,1024]{1,0:T(8,128)S(1)}) fusion(f32[512,128]{1,0:T(8,128)S(1)} %copy-done, f32[1024,128]{1,0:T(8,128)S(1)} %copy-done.1, f32[1024]{0:T(1024)S(1)} %multiply_reduce_fusion, f32[512]{0:T(512)S(1)} %multiply_reduce_fusion.4), kind=kOutput, calls=%fused_computation.33 | convolution fusion | flops 807927296 | bytes 2891776 | tf_op jit(solution)/shard_map/dot_general | solution.py:11
  46.6 1.8 fusion.12
  48.5 2.5 %fusion.9 = f32[512,128]{1,0:T(8,128)} fusion(f32[512,128]{1,0:T(8,128)S(1)} %fusion.12, f32[512,1024]{1,0:T(8,128)S(1)} %get-tuple-element.9, f32[1024,128]{1,0:T(8,128)S(1)} %copy-done.1, f32[512,128]{1,0:T(8,128)S(1)} %copy-done, f32[512]{0:T(512)S(1)} %get-tuple-element.8), kind=kOutput, calls=%fused_computation.15 | convolution fusion | flops 805568512 | bytes 3409920 | tf_op jit(solution)/shard_map/dot_general | solution.py:20
  50.9 0.0 all-gather.5.cloned.1.call-update
  51.0 0.0 all-gather.7.cloned.1.call-start
  51.0 64.6 %all-gather.5.cloned.1.call-done = f32[8192,128]{1,0:T(8,128)} async-done(((f32[512,128]{1,0:T(8,128)}), f32[8192,128]{1,0:T(8,128)}) %all-gather.5.cloned.1.call-update) | async-done | bytes 4194320 | tf_op jit(solution)/shard_map/all_gather | solution.py:46
  115.6 2.4 %reduce_sum.116 = f32[512,128]{1,0:T(8,128)S(1)} reduce(f32[16,512,128]{2,1,0:T(8,128)} %bitcast.26, f32[]{:T(128)} %constant.10.clone.1), dimensions={0}, to_apply=%region_5.0 | reduce | flops 983040 | bytes 4456452 | tf_op jit(solution)/shard_map/reduce_sum | solution.py:46
  118.0 0.1 multiply_reduce_fusion.2
  118.2 27.3 %all_gather.21 = f32[512,128]{1,0:T(8,128)S(1)} all-gather(f32[32,128]{1,0:T(8,128)S(1)} %constant_dynamic-slice_fusion), channel_id=1, replica_groups=mesh['dom'=16,'ref'=16] {'dom'}, dimensions={0}, use_global_device_ids=true | all-gather | bytes 278528 | tf_op jit(solution)/shard_map/all_gather | solution.py:27
  145.5 0.1 multiply_reduce_fusion.1
  145.6 2.3 %fusion.18 = (f32[512]{0:T(512)S(1)}, f32[512,1024]{1,0:T(8,128)S(1)}) fusion(f32[512,128]{1,0:T(8,128)S(1)} %get-tuple-element.5, f32[1024,128]{1,0:T(8,128)S(1)} %copy-done.1, f32[1024]{0:T(1024)S(1)} %multiply_reduce_fusion, f32[512]{0:T(512)S(1)} %get-tuple-element.4), kind=kOutput, calls=%fused_computation.35 | convolution fusion | flops 807927296 | bytes 2891776 | tf_op jit(solution)/shard_map/dot_general | solution.py:11
  147.9 1.2 fusion.17
  149.1 1.8 fusion.11
  150.9 2.5 %fusion.10 = f32[512,128]{1,0:T(8,128)} fusion(f32[512,128]{1,0:T(8,128)S(1)} %fusion.11, f32[512,1024]{1,0:T(8,128)S(1)} %get-tuple-element.13, f32[1024,128]{1,0:T(8,128)S(1)} %copy-done.1, f32[512,128]{1,0:T(8,128)S(1)} %get-tuple-element.5, f32[512]{0:T(512)S(1)} %get-tuple-element.12), kind=kOutput, calls=%fused_computation.16 | convolution fusion | flops 805568512 | bytes 3409920 | tf_op jit(solution)/shard_map/dot_general | solution.py:20
  153.4 0.0 all-gather.7.cloned.1.call-update
  153.4 63.2 %all-gather.7.cloned.1.call-done = f32[8192,128]{1,0:T(8,128)} async-done(((f32[512,128]{1,0:T(8,128)}), f32[8192,128]{1,0:T(8,128)}) %all-gather.7.cloned.1.call-update) | async-done | bytes 4194320 | tf_op jit(solution)/shard_map/all_gather | solution.py:46
  216.6 2.4 %reduce_sum.121 = f32[512,128]{1,0:T(8,128)S(1)} reduce(f32[16,512,128]{2,1,0:T(8,128)} %bitcast.27, f32[]{:T(128)} %constant.10.clone.1), dimensions={0}, to_apply=%region_10.0 | reduce | flops 983040 | bytes 4456452 | tf_op jit(solution)/shard_map/reduce_sum | solution.py:46
  219.0 0.6 subtract_multiply_fusion
  (1 shorter events, 0.0 us)
Async XLA Ops:
  7.2 37.2 %copy-start = (f32[512,128]{1,0:T(8,128)S(1)}, f32[512,128]{1,0:T(8,128)}, u32[]{:S(2)}) copy-start(f32[512,128]{1,0:T(8,128)} %param.2) | copy-start | bytes 786436
  7.2 37.2 %copy-start.1 = (f32[1024,128]{1,0:T(8,128)S(1)}, f32[1024,128]{1,0:T(8,128)}, u32[]{:S(2)}) copy-start(f32[1024,128]{1,0:T(8,128)} %param.3) | copy-start | bytes 1572868
  7.2 108.4 %all-gather.5.cloned.1.call-start = ((), (), s32[]{:S(2)}) async-start(), calls=%async_computation | async-start | bytes 4456448 | tf_op jit(solution)/shard_map/all_gather | solution.py:46
  51.0 165.6 %all-gather.7.cloned.1.call-start = ((), (), s32[]{:S(2)}) async-start(), calls=%async_computation.1 | async-start | bytes 4456448 | tf_op jit(solution)/shard_map/all_gather | solution.py:46
Sparse Core Ops, SparseCore 0:
  51.1 64.4 all-gather.4
  153.5 63.0 all-gather.6
